TPU v7x, 128 devices: a whole 4x4x4 slice. The times are simulated.
128 devices in a mesh: row: 8 (over x, core), col: 16 (over y, z).
Axes of the slice: x: 4, y: 4, z: 4, core: 2. Of those that a mesh axis runs over, the one named last changes fastest.
Arguments:
- valence: bfloat16 [2, 16, 32768], replicated, may hold values from -6 to 6
- conduction: bfloat16 [2, 128, 32768], replicated, may hold values from -6 to 6
- valence_energy: float32 [16], replicated, may hold values from -8 to -1
- conduction_energy: float32 [128], replicated, may hold values from 0.5 to 6
- band_pairs: int32 [1024, 2], P(('row', 'col')), may hold values from 0 to 127, as said below
- grid_index: int32 [16384], replicated, may hold values from 0 to 32767, as said below
Outputs:
- response: float32 [2, 16384, 16384], P(None, 'row', 'col')
Inputs may be any that keep to these rules, and one draw needn't show every extreme that they name: `band_pairs`: the rows are distinct combinations of a valence band below 16 and a conduction band below 128, half of all combinations. `grid_index`: the 16384 entries are distinct.
All inputs are finite; a program needn't handle non-finite values.
Results may differ from a plain program's by a relative error of at most 0.0039.
Values may be sent and summed in bfloat16 or wider, within the bound.
A program may use at most 192 MiB of HBM per device.

v0:
```python
import math
import jax
import jax.numpy as jnp
from jax import lax
from jax.sharding import PartitionSpec as P

N1 = 32
N2 = 32
N3 = 32
NVB = 16
NCB = 128


def tables(length):
    position = jnp.arange(length, dtype=jnp.int32)
    phase_angle = (position[:, None] * position[None, :] % length).astype(jnp.float32) * (
        2.0 * math.pi / length
    )
    return (jnp.cos(phase_angle), jnp.sin(phase_angle))


def plane_table():
    plane_size = N2 * N3
    position = jnp.arange(plane_size, dtype=jnp.int32)
    second = position // N3
    third = position % N3
    phase_index = (
        second[:, None] * second[None, :] % N2 * N3 + third[:, None] * third[None, :] % N3 * N2
    )
    phase_angle = (phase_index % plane_size).astype(jnp.float32) * (2.0 * math.pi / plane_size)
    cosine = jnp.cos(phase_angle)
    sine_table = jnp.sin(phase_angle)
    upper = jnp.concatenate([cosine, -sine_table], axis=1)
    lower = jnp.concatenate([sine_table, cosine], axis=1)
    return jnp.concatenate([upper, lower], axis=0)


def transform(rho_real, rho_imag):
    pair_count = rho_real.shape[0]
    plane_size = N2 * N3
    stacked = jnp.concatenate(
        [
            rho_real.reshape(pair_count, N1, plane_size),
            rho_imag.reshape(pair_count, N1, plane_size),
        ],
        axis=2,
    )
    plane = jnp.dot(
        stacked.reshape(pair_count * N1, 2 * plane_size),
        plane_table(),
        precision=lax.Precision.HIGHEST,
    )
    plane = plane.reshape(pair_count, N1, 2 * plane_size)
    cosine, sine_table = tables(N1)
    cos_part = jnp.einsum("kr,prx->pkx", cosine, plane, precision=lax.Precision.HIGHEST)
    sin_part = jnp.einsum("kr,prx->pkx", sine_table, plane, precision=lax.Precision.HIGHEST)
    out_real = cos_part[:, :, :plane_size] + sin_part[:, :, plane_size:]
    out_imag = cos_part[:, :, plane_size:] - sin_part[:, :, :plane_size]
    return (out_real.reshape(pair_count, -1), out_imag.reshape(pair_count, -1))


def pair_spectrum(valence, conduction, valence_energy, conduction_energy, band_pairs):
    valence_rows = jnp.take(valence, band_pairs[:, 0], axis=1).astype(jnp.float32)
    conduction_rows = jnp.take(conduction, band_pairs[:, 1], axis=1).astype(jnp.float32)
    rho_real = valence_rows[0] * conduction_rows[0] + valence_rows[1] * conduction_rows[1]
    rho_imag = valence_rows[0] * conduction_rows[1] - valence_rows[1] * conduction_rows[0]
    out_real, out_imag = transform(rho_real, rho_imag)
    normalize = 1.0 / math.sqrt(N1 * N2 * N3)
    spectrum = jnp.stack([out_real, out_imag]) * normalize
    valence_hot = (
        band_pairs[:, 0][:, None] == jnp.arange(valence_energy.shape[0], dtype=jnp.int32)[None, :]
    )
    conduction_hot = (
        band_pairs[:, 1][:, None]
        == jnp.arange(conduction_energy.shape[0], dtype=jnp.int32)[None, :]
    )
    energy_gap = jnp.sum(jnp.where(valence_hot, valence_energy[None, :], 0.0), axis=1) - jnp.sum(
        jnp.where(conduction_hot, conduction_energy[None, :], 0.0), axis=1
    )
    weights = 2.0 / (math.sqrt(NVB * NCB // 2) * energy_gap)
    return (spectrum, weights)


def contract(weighted_part, operand, left_dims, right_dims):
    full_left = (0,) + tuple((d + 1 for d in left_dims))
    full_right = (0,) + tuple((d + 1 for d in right_dims))
    real_part = lax.dot_general(
        weighted_part,
        operand,
        ((full_left, full_right), ((), ())),
        preferred_element_type=jnp.float32,
    )
    pair_dims = ((left_dims, right_dims), ((), ()))
    imag_part = lax.dot_general(
        weighted_part[0], operand[1], pair_dims, preferred_element_type=jnp.float32
    ) - lax.dot_general(weighted_part[1], operand[0], pair_dims, preferred_element_type=jnp.float32)
    return jnp.stack([real_part, imag_part])


def body(valence, conduction, valence_energy, conduction_energy, band_pairs, grid_index):
    spectrum, weights = pair_spectrum(
        valence, conduction, valence_energy, conduction_energy, band_pairs
    )
    row_count = lax.axis_size("row")
    column_count = lax.axis_size("col")
    selected = jnp.take(spectrum, grid_index, axis=2)
    weighted = (weights[None, :, None] * selected).astype(jnp.bfloat16)
    density = selected.astype(jnp.bfloat16)
    weighted_block = lax.all_to_all(weighted, "row", split_axis=2, concat_axis=1, tiled=True)
    density_block = lax.all_to_all(density, "col", split_axis=2, concat_axis=1, tiled=True)
    weighted_all = lax.all_gather(weighted_block, "col", axis=1, tiled=True)
    density_all = lax.all_gather(density_block, "row", axis=1, tiled=True)
    pair_count = density_all.shape[1]
    per_device = pair_count // (row_count * column_count)
    weighted_split = weighted_all.reshape(
        2, column_count, row_count, per_device, weighted_all.shape[2]
    )
    density_split = density_all.reshape(
        2, row_count, column_count, per_device, density_all.shape[2]
    )
    return contract(weighted_split, density_split, (0, 1, 2), (1, 0, 2))


def solution(mesh):
    return jax.shard_map(
        body,
        mesh=mesh,
        in_specs=(P(), P(), P(), P(), P(("row", "col"), None), P()),
        out_specs=P(None, "row", "col"),
        check_vma=False,
    )
```

profile of v0, /device:TPU:1, one launch (start us, length us, event | category | flops | bytes accessed | tf_op | source)
XLA Modules:
  0.0 724.0 jit_solution(14251131210681987142)
XLA Ops:
  6.5 0.0 all-gather.5.cloned.1.call-start
  6.5 0.8 fusion.55
  7.4 0.8 and_bitcast_fusion.1
  8.2 3.6 gather_fusion.1
  11.8 1.5 convert_bitcast_fusion.1
  13.3 0.0 copy-done
  13.3 3.5 gather_fusion
  16.9 0.0 copy-start.2
  16.9 0.2 convert_bitcast_fusion.2
  17.1 1.4 copy-done.2
  18.4 0.3 multiply_add_fusion
  18.8 0.6 copy.50
  19.4 0.6 copy.51
  20.0 23.7 %fusion.25 = (f32[1024,1024]{1,0:T(8,128)}, f32[1024,1024]{1,0:T(8,128)}, f32[1024,1024]{1,0:T(8,128)}) fusion(s32[1024]{0:T(1024)S(1)} %get-tuple-element.24, s32[1024]{0:T(1024)S(1)} %get-tuple-element.25), kind=kLoop, calls=%fused_computation.53 | loop fusion | flops 41943040 | bytes 12591104 | tf_op jit(solution)/shard_map/neg | solution.py:33
  43.7 22.3 %fusion = f32[8,32,2048]{2,1,0:T(8,128)} fusion(f32[1024,1024]{1,0:T(8,128)} %get-tuple-element.15, f32[1024,1024]{1,0:T(8,128)} %get-tuple-element.14, f32[1024,1024]{1,0:T(8,128)} %get-tuple-element.13, f32[8,32,1024]{2,1,0:T(8,128)S(1)} %bitcast.102, f32[8,32,1024]{2,1,0:T(8,128)S(1)} %bitcast.103), kind=kOutput, calls=%fused_computation.4 | convolution fusion | flops 12898009088 | bytes 16777216 | tf_op jit(solution)/shard_map/dot_general | solution.py:48
  66.0 3.8 convolution_bitcast_fusion.1
  69.9 2.1 convolution_bitcast_fusion.2
  72.0 1.4 slice_add_fusion
  73.4 2.4 stack_reshape.6
  75.8 1.2 stack_reshape.7
  77.0 1.7 maximum_multiply_fusion
  78.7 28.8 %copy.31 = f32[2,8,32768]{1,0,2:T(2,128)} copy(f32[2,8,32768]{2,1,0:T(8,128)S(1)} %maximum_multiply_fusion) | data formatting | bytes 4194304 | tf_op jit(solution)/shard_map/mul | solution.py:69
  107.5 251.9 %gather_fusion.2 = f32[16384,2,8]{2,1,0:T(2,128)} fusion(f32[2,8,32768]{1,0,2:T(2,128)} %copy.31, s32[16384]{0:T(1024)S(1)} %fusion.26), kind=kCustom, calls=%fused_computation.2 | custom fusion | bytes 2162688 | tf_op jit(solution)/shard_map/jit(_take)/gather | solution.py:106
  359.4 71.1 %fusion.59 = bf16[16384,2,8]{2,1,0:T(2,128)(2,1)} fusion(f32[16384,2,8]{2,1,0:T(2,128)} %gather_fusion.2, pred[16384]{0:T(1024)(128)(4,1)S(1)} %compare_and_fusion), kind=kLoop, calls=%fused_computation.113 | loop fusion | flops 262144 | bytes 1589248
  430.5 10.5 %reshape.154 = bf16[16,2,8192]{2,1,0:T(2,128)(2,1)S(1)} reshape(bf16[16384,2,8]{2,1,0:T(2,128)(2,1)} %fusion.59) | data formatting | bytes 1048576
  440.9 18.7 %all_to_all.36 = bf16[16,2,8192]{2,1,0:T(2,128)(2,1)S(1)} all-to-all(bf16[16,2,8192]{2,1,0:T(2,128)(2,1)S(1)} %reshape.154), channel_id=1, replica_groups=mesh['row'=8,'col'=16] {'col'}, dimensions={0} | all-to-all | bytes 1048576 | tf_op jit(solution)/shard_map/all_to_all | solution.py:110
  459.6 10.9 %reshape.155 = bf16[16384,2,8]{2,1,0:T(2,128)(2,1)} reshape(bf16[16,2,8192]{2,1,0:T(2,128)(2,1)S(1)} %all_to_all.36) | data formatting | bytes 1048576
  470.6 19.3 %copy.33 = bf16[2,16,8,1024]{3,2,1,0:T(8,128)(2,1)} copy(bf16[2,16,8,1024]{2,0,3,1:T(2,128)(2,1)} %bitcast.90) | data formatting | bytes 1048576 | tf_op jit(solution)/shard_map/all_to_all | solution.py:110
  489.8 0.0 all-gather.5.cloned.1.call-update
  489.8 0.0 all-gather.3.cloned.1.call-start
  489.9 0.2 select_reduce_fusion
  490.1 0.2 select_reduce_fusion.1
  490.3 59.2 %fusion.60 = bf16[16384,2,8]{2,1,0:T(2,128)(2,1)} fusion(f32[16384,2,8]{2,1,0:T(2,128)} %gather_fusion.2, pred[16384]{0:T(1024)(128)(4,1)S(1)} %compare_and_fusion, f32[8]{0:T(128)S(1)} %multiply_divide_fusion), kind=kLoop, calls=%fused_computation.114 | loop fusion | flops 786432 | bytes 1589280
  549.4 10.4 %reshape.152 = bf16[8,2,16384]{2,1,0:T(2,128)(2,1)S(1)} reshape(bf16[16384,2,8]{2,1,0:T(2,128)(2,1)} %fusion.60) | data formatting | bytes 1048576
  559.9 15.6 %all_to_all.37 = bf16[8,2,16384]{2,1,0:T(2,128)(2,1)S(1)} all-to-all(bf16[8,2,16384]{2,1,0:T(2,128)(2,1)S(1)} %reshape.152), channel_id=1, replica_groups=mesh['row'=8,'col'=16] {'row'}, dimensions={0} | all-to-all | bytes 1048576 | tf_op jit(solution)/shard_map/all_to_all | solution.py:109
  575.5 10.9 %reshape.153 = bf16[16384,2,8]{2,1,0:T(2,128)(2,1)} reshape(bf16[8,2,16384]{2,1,0:T(2,128)(2,1)S(1)} %all_to_all.37) | data formatting | bytes 1048576
  586.3 19.2 %copy.32 = bf16[2,8,8,2048]{3,2,1,0:T(8,128)(2,1)} copy(bf16[2,8,8,2048]{2,0,3,1:T(2,128)(2,1)} %bitcast.91) | data formatting | bytes 1048576 | tf_op jit(solution)/shard_map/all_to_all | solution.py:109
  605.5 0.0 all-gather.3.cloned.1.call-update
  605.5 0.0 all-gather.5.cloned.1.call-done
  605.6 4.7 fusion.58
  610.2 62.7 %all-gather.3.cloned.1.call-done = bf16[2,1024,2048]{2,1,0:T(8,128)(2,1)} async-done(((bf16[2,64,2048]{2,1,0:T(8,128)(2,1)}), bf16[2,1024,2048]{2,1,0:T(8,128)(2,1)}) %all-gather.3.cloned.1.call-update) | async-done | bytes 8388624 | tf_op jit(solution)/shard_map/all_gather | solution.py:111
  672.9 14.5 %convolution_bitcast_fusion = f32[1,2048,1024]{2,1,0:T(8,128)} fusion(bf16[2,16,8,8,2048]{4,3,2,1,0:T(8,128)(2,1)} %bitcast.92, bf16[2,8,16,8,1024]{4,3,2,1,0:T(8,128)(2,1)} %bitcast.93), kind=kOutput, calls=%fused_computation.31 | convolution fusion | flops 8589934592 | bytes 20971520 | tf_op jit(solution)/shard_map/dot_general | solution.py:87
  687.4 5.4 fusion.57
  692.8 0.0 copy-done.6
  692.8 6.9 fusion.21
  699.8 7.4 %fusion.8 = f32[1,2048,1024]{2,1,0:T(8,128)S(1)} fusion(f32[2048,1024,1,1]{1,0,3,2:T(8,128)} %fusion.21, bf16[16,8,8,2048]{3,2,1,0:T(8,128)(2,1)S(1)} %bitcast.96, bf16[8,16,8,1024]{3,2,1,0:T(8,128)(2,1)S(1)} %bitcast.100), kind=kOutput, calls=%fused_computation.16 | convolution fusion | flops 4297064448 | bytes 23068672 | tf_op jit(solution)/shard_map/dot_general | solution.py:96
  707.1 0.0 copy-start.1
  707.2 10.0 %pad_maximum_fusion = f32[2,2048,1024]{2,1,0:T(8,128)} fusion(f32[1,2048,1024]{2,1,0:T(8,128)S(1)} %fusion.8, f32[1,2048,1024]{2,1,0:T(8,128)} %convolution_bitcast_fusion), kind=kLoop, calls=%fused_computation.11 | loop fusion | flops 4194304 | bytes 33554432 | tf_op jit(solution)/shard_map/stack | solution.py:97
  (20 shorter events, 0.1 us)
Async XLA Ops:
  6.5 6.8 copy-start
  6.5 599.0 %all-gather.5.cloned.1.call-start = ((), (), s32[]{:S(2)}) async-start(), calls=%async_computation.3 | async-start | bytes 4718592 | tf_op jit(solution)/shard_map/all_gather | solution.py:112
  16.9 1.6 copy-start.2
  66.0 3.8 copy-start.3
  66.0 6.0 copy-start.7
  470.6 19.3 %copy-start.8 = (f32[128]{0:T(128)S(1)}, f32[128]{0:T(128)}, u32[]{:S(2)}) copy-start(f32[128]{0:T(128)} %param.9) | copy-start | bytes 1540
  470.6 19.5 %copy-start.9 = (f32[16]{0:T(128)S(1)}, f32[16]{0:T(128)}, u32[]{:S(2)}) copy-start(f32[16]{0:T(128)} %param.8) | copy-start | bytes 196
  489.8 183.1 %all-gather.3.cloned.1.call-start = ((), (), s32[]{:S(2)}) async-start(), calls=%async_computation.2 | async-start | bytes 8912896 | tf_op jit(solution)/shard_map/all_gather | solution.py:111
  687.4 5.4 copy-start.6
  692.8 7.0 copy-start.4
  692.8 7.0 copy-start.5
  707.1 10.0 %copy-start.1 = (bf16[2,16,32768]{2,1,0:T(8,128)(2,1)S(1)}, bf16[2,16,32768]{2,1,0:T(8,128)(2,1)}, u32[]{:S(2)}) copy-start(bf16[2,16,32768]{2,1,0:T(8,128)(2,1)} %param.6) | copy-start | bytes 6291460
Sparse Core Ops, SparseCore 0:
  490.0 31.7 all-gather.4
  605.7 67.1 all-gather.2
where the time goes:
time: 734 us; the launch traced here: 724 us
  local copies, waits for them, and re-layouts  385 us (52%)
  other arithmetic  171 us (23%)
  waiting for transfers between devices  62.7 us (9%)
  matrix products  57 us (8%)
  blocking collectives  34.3 us (5%)
  between operations  13.6 us (2%)
    gather x1, local copies, waits for them, and re-layouts, body(): selected = jnp.take(spectrum, grid_index, axis=2)  252 us
    unnamed x2, other arithmetic  130 us
    all_gather x1, waiting for transfers between devices, body(): weighted_all = lax.all_gather(weighted_block, 'col', axis=1, tiled=True)  62.7 us
    unnamed x26, local copies, waits for them, and re-layouts  45.3 us
    mul x1, local copies, waits for them, and re-layouts, pair_spectrum(): spectrum = jnp.stack([out_real, out_imag]) * normalize  28.8 us
    neg x1, other arithmetic, plane_table(): upper = jnp.concatenate([cosine, -sine_table], axis=1)  23.7 us
    dot_general x1, matrix products, transform(): jnp.dot(stacked.reshape(pair_count * N1, 2 * plane_size), plane_table(),...  22.3 us
    all_to_all x1, local copies, waits for them, and re-layouts, body(): lax.all_to_all(density, 'col', split_axis=2, concat_axis=1, tiled=True)  19.3 us
  transfers between devices with their start and end apart: 2, of which 1 were waited for; matrix products, arithmetic and copies ran while one was open for 14% of the time, Pallas kernels for 0%

commit v1 on v0

--- a/solution.py
+++ b/solution.py
@@ -108,7 +108,15 @@
     density = selected.astype(jnp.bfloat16)
     weighted_block = lax.all_to_all(weighted, "row", split_axis=2, concat_axis=1, tiled=True)
     density_block = lax.all_to_all(density, "col", split_axis=2, concat_axis=1, tiled=True)
-    weighted_all = lax.all_gather(weighted_block, "col", axis=1, tiled=True)
+    weighted_all = jnp.concatenate(
+        jax.lax.all_to_all(
+            jnp.stack([weighted_block for _ in range(jax.lax.axis_size("col"))]),
+            axis_name="col",
+            split_axis=0,
+            concat_axis=0,
+        ),
+        1,
+    )
     density_all = lax.all_gather(density_block, "row", axis=1, tiled=True)
     pair_count = density_all.shape[1]
     per_device = pair_count // (row_count * column_count)

time: 734 us -> 789 us (1.075)
  waiting for transfers between devices: 62.7 us -> 111 us
  blocking collectives: 34.3 us -> 0 us
  local copies, waits for them, and re-layouts: 385 us -> 406 us
  starting transfers between devices: 0.04 us -> 20.3 us
    all_to_all x0 -> x3, waiting for transfers between devices: none -> 76.5 us  [the longest x1 76.5 us: body(): jax.lax.all_to_all(jnp.stack([weighted_block for _ in range(jax.lax.axis_...]
    all_gather x1 -> x0, waiting for transfers between devices: 62.7 us -> none  [body(): weighted_all = lax.all_gather(weighted_block, 'col', axis=1, tiled=True)]
    all_gather x1, waiting for transfers between devices: 0.02 us -> 34.8 us  [body(): density_all = lax.all_gather(density_block, 'row', axis=1, tiled=True)]
    all_to_all x2 -> x0, blocking collectives: 34.3 us -> none  [the longest x1 18.7 us: body(): lax.all_to_all(density, 'col', split_axis=2, concat_axis=1, tiled=True)]
    all_to_all x0 -> x3, starting transfers between devices: none -> 20.3 us  [the longest x1 7.77 us: body(): lax.all_to_all(density, 'col', split_axis=2, concat_axis=1, tiled=True)]
    reshape x0 -> x1, local copies, waits for them, and re-layouts: none -> 11.4 us  [body(): jnp.concatenate(jax.lax.all_to_all(jnp.stack([weighted_block for _ in ran...]
    unnamed x26 -> x34, local copies, waits for them, and re-layouts: 45.3 us -> 46.8 us
    unnamed x2 -> x3, other arithmetic: 130 us -> 131 us
  transfers between devices with their start and end apart: 2 -> 4, of which waited for: 1 -> 2; matrix products, arithmetic and copies ran while one was open for 14% -> 17% of each run, Pallas kernels for 0% -> 0%
where the time goes in v1:
time: 789 us; the launch traced here: 778 us
  local copies, waits for them, and re-layouts  406 us (51%)
  other arithmetic  168 us (21%)
  waiting for transfers between devices  111 us (14%)
  matrix products  57.7 us (7%)
  starting transfers between devices  20.3 us (3%)
  between operations  14 us (2%)
    gather x1, local copies, waits for them, and re-layouts, body(): selected = jnp.take(spectrum, grid_index, axis=2)  252 us
    unnamed x3, other arithmetic  131 us
    all_to_all x1, waiting for transfers between devices, body(): jax.lax.all_to_all(jnp.stack([weighted_block for _ in range(jax.lax.axis_...  76.5 us
    unnamed x34, local copies, waits for them, and re-layouts  46.8 us
    all_gather x1, waiting for transfers between devices, body(): density_all = lax.all_gather(density_block, 'row', axis=1, tiled=True)  34.8 us
    mul x1, local copies, waits for them, and re-layouts, pair_spectrum(): spectrum = jnp.stack([out_real, out_imag]) * normalize  29 us
    neg x1, other arithmetic, plane_table(): upper = jnp.concatenate([cosine, -sine_table], axis=1)  23.7 us
    dot_general x1, matrix products, transform(): jnp.dot(stacked.reshape(pair_count * N1, 2 * plane_size), plane_table(),...  22.3 us
  transfers between devices with their start and end apart: 4, of which 2 were waited for; matrix products, arithmetic and copies ran while one was open for 17% of the time, Pallas kernels for 0%

profile of v1, /device:TPU:1, one launch (start us, length us, event | category | flops | bytes accessed | tf_op | source)
XLA Modules:
  0.0 777.7 jit_solution(13077495643563549349)
XLA Ops:
  6.5 0.8 fusion.55
  7.4 0.8 and_bitcast_fusion.1
  8.2 3.6 gather_fusion.1
  11.8 1.5 convert_bitcast_fusion.1
  13.3 3.5 gather_fusion
  16.9 0.2 convert_bitcast_fusion.2
  17.1 1.4 copy-done.2
  18.4 0.3 multiply_add_fusion
  18.8 0.6 copy.62
  19.4 0.6 copy.63
  20.0 23.7 %fusion.25 = (f32[1024,1024]{1,0:T(8,128)}, f32[1024,1024]{1,0:T(8,128)}, f32[1024,1024]{1,0:T(8,128)}) fusion(s32[1024]{0:T(1024)S(1)} %get-tuple-element.24, s32[1024]{0:T(1024)S(1)} %get-tuple-element.25), kind=kLoop, calls=%fused_computation.53 | loop fusion | flops 41943040 | bytes 12591104 | tf_op jit(solution)/shard_map/neg | solution.py:33
  43.7 22.3 %fusion = f32[8,32,2048]{2,1,0:T(8,128)} fusion(f32[1024,1024]{1,0:T(8,128)} %get-tuple-element.15, f32[1024,1024]{1,0:T(8,128)} %get-tuple-element.14, f32[1024,1024]{1,0:T(8,128)} %get-tuple-element.13, f32[8,32,1024]{2,1,0:T(8,128)S(1)} %bitcast.105, f32[8,32,1024]{2,1,0:T(8,128)S(1)} %bitcast.106), kind=kOutput, calls=%fused_computation.4 | convolution fusion | flops 12898009088 | bytes 16777216 | tf_op jit(solution)/shard_map/dot_general | solution.py:48
  66.0 3.8 convolution_bitcast_fusion.1
  69.8 2.1 convolution_bitcast_fusion.2
  72.0 1.4 slice_add_fusion
  73.3 2.4 stack_reshape.6
  75.8 1.2 stack_reshape.7
  76.9 1.7 maximum_multiply_fusion
  78.7 29.0 %copy.40 = f32[2,8,32768]{1,0,2:T(2,128)} copy(f32[2,8,32768]{2,1,0:T(8,128)S(1)} %maximum_multiply_fusion) | data formatting | bytes 4194304 | tf_op jit(solution)/shard_map/mul | solution.py:69
  107.6 252.1 %gather_fusion.2 = f32[16384,2,8]{2,1,0:T(2,128)} fusion(f32[2,8,32768]{1,0,2:T(2,128)} %copy.40, s32[16384]{0:T(1024)S(1)} %fusion.26), kind=kCustom, calls=%fused_computation.2 | custom fusion | bytes 2162688 | tf_op jit(solution)/shard_map/jit(_take)/gather | solution.py:106
  359.7 0.2 select_reduce_fusion
  359.9 0.2 select_reduce_fusion.1
  360.1 71.7 %fusion.60 = bf16[16384,2,8]{2,1,0:T(2,128)(2,1)} fusion(f32[16384,2,8]{2,1,0:T(2,128)} %gather_fusion.2, pred[16384]{0:T(1024)(128)(4,1)S(1)} %compare_and_fusion, f32[8]{0:T(128)S(1)} %multiply_divide_fusion), kind=kLoop, calls=%fused_computation.114 | loop fusion | flops 786432 | bytes 1589280
  431.8 11.2 %reshape.155 = bf16[8,2,16384]{2,1,0:T(2,128)(2,1)} reshape(bf16[16384,2,8]{2,1,0:T(2,128)(2,1)} %fusion.60) | data formatting | bytes 1048576
  443.0 5.8 all-to-all-start
  448.8 59.1 %fusion.59 = bf16[16384,2,8]{2,1,0:T(2,128)(2,1)} fusion(f32[16384,2,8]{2,1,0:T(2,128)} %gather_fusion.2, pred[16384]{0:T(1024)(128)(4,1)S(1)} %compare_and_fusion), kind=kLoop, calls=%fused_computation.113 | loop fusion | flops 262144 | bytes 1589248
  507.9 11.2 %reshape.157 = bf16[16,2,8192]{2,1,0:T(2,128)(2,1)} reshape(bf16[16384,2,8]{2,1,0:T(2,128)(2,1)} %fusion.59) | data formatting | bytes 1048576
  519.1 7.8 all-to-all-start.2
  526.8 10.9 %reshape.156 = bf16[16384,2,8]{2,1,0:T(2,128)(2,1)} reshape(bf16[8,2,16384]{2,1,0:T(2,128)(2,1)S(1)} %all-to-all-done) | data formatting | bytes 1048576
  537.7 17.7 %copy.41 = bf16[2,8,8,2048]{3,1,2,0:T(8,128)(2,1)S(1)} copy(bf16[2,8,8,2048]{1,0,3,2:T(2,128)(2,1)} %bitcast.91) | data formatting | bytes 1048576 | tf_op jit(solution)/shard_map/all_to_all | solution.py:109
  555.4 4.5 stack.14
  559.9 6.7 all-to-all-start.1
  566.6 0.0 all-gather.2.cloned.1.call-start
  566.6 10.9 %reshape.158 = bf16[16384,2,8]{2,1,0:T(2,128)(2,1)} reshape(bf16[16,2,8192]{2,1,0:T(2,128)(2,1)S(1)} %all-to-all-done.2) | data formatting | bytes 1048576
  577.5 19.2 %copy.43 = bf16[2,16,8,1024]{3,2,1,0:T(8,128)(2,1)} copy(bf16[2,16,8,1024]{2,0,3,1:T(2,128)(2,1)} %bitcast.92) | data formatting | bytes 1048576 | tf_op jit(solution)/shard_map/all_to_all | solution.py:110
  596.7 0.0 all-gather.2.cloned.1.call-update
  596.7 34.8 %all-gather.2.cloned.1.call-done = bf16[2,1024,1024]{2,1,0:T(8,128)(2,1)} async-done(((bf16[2,128,1024]{2,1,0:T(8,128)(2,1)}), bf16[2,1024,1024]{2,1,0:T(8,128)(2,1)}) %all-gather.2.cloned.1.call-update) | async-done | bytes 4194320 | tf_op jit(solution)/shard_map/all_gather | solution.py:120
  631.5 4.6 fusion.58
  636.1 76.5 %all-to-all-done.1 = bf16[16,2,64,2048]{3,2,1,0:T(8,128)(2,1)} async-done(((bf16[16,2,64,2048]{3,2,1,0:T(8,128)(2,1)}), bf16[16,2,64,2048]{3,2,1,0:T(8,128)(2,1)}, u32[]{:S(2)}, u32[]{:S(2)}) %all-to-all-start.1) | async-done | bytes 8388640 | tf_op jit(solution)/shard_map/all_to_all | solution.py:112
  712.7 11.4 %copy.42 = bf16[2,16,64,2048]{3,1,2,0:T(8,128)(2,1)} copy(bf16[2,16,64,2048]{3,2,0,1:T(8,128)(2,1)} %bitcast.17) | data formatting | bytes 16777216 | tf_op jit(solution)/shard_map/reshape | solution.py:111
  724.1 3.8 fusion.57
  727.9 0.0 slice-start
  727.9 2.3 copy.45
  730.2 4.2 copy.47
  734.5 12.4 %convolution_bitcast_fusion = f32[1,2048,1024]{2,1,0:T(8,128)} fusion(bf16[2,16,8,8,2048]{4,1,3,2,0:T(8,128)(2,1)S(1)} %bitcast.95, bf16[2,8,16,8,1024]{4,3,2,1,0:T(8,128)(2,1)S(1)} %bitcast.96), kind=kOutput, calls=%fused_computation.31 | convolution fusion | flops 8589934592 | bytes 20971520 | tf_op jit(solution)/shard_map/dot_general | solution.py:87
  746.9 7.3 fusion.21
  754.2 9.8 %fusion.8 = f32[1,2048,1024]{2,1,0:T(8,128)S(1)} fusion(f32[2048,1024,1,1]{1,0,3,2:T(8,128)} %fusion.21, bf16[16,8,8,2048]{3,0,2,1:T(8,128)(2,1)S(1)} %bitcast.97, bf16[8,16,8,1024]{3,2,1,0:T(8,128)(2,1)S(1)} %bitcast.103), kind=kOutput, calls=%fused_computation.16 | convolution fusion | flops 4297064448 | bytes 23068672 | tf_op jit(solution)/shard_map/dot_general | solution.py:96
  764.1 6.4 pad_maximum_fusion
  (34 shorter events, 0.1 us)
Async XLA Ops:
  6.5 6.8 copy-start
  16.9 1.6 copy-start.2
  66.0 3.8 copy-start.3
  66.0 5.9 copy-start.9
  78.7 281.0 %copy-start.10 = (f32[128]{0:T(128)S(1)}, f32[128]{0:T(128)}, u32[]{:S(2)}) copy-start(f32[128]{0:T(128)} %param.9) | copy-start | bytes 1540
  78.7 281.2 %copy-start.11 = (f32[16]{0:T(128)S(1)}, f32[16]{0:T(128)}, u32[]{:S(2)}) copy-start(f32[16]{0:T(128)} %param.8) | copy-start | bytes 196
  443.0 76.1 %all-to-all-start = ((bf16[8,2,16384]{2,1,0:T(2,128)(2,1)}), bf16[8,2,16384]{2,1,0:T(2,128)(2,1)S(1)}, u32[]{:S(2)}, u32[]{:S(2)}) async-start(bf16[8,2,16384]{2,1,0:T(2,128)(2,1)} %reshape.155), calls=%async_computation | async-start | bytes 1048576 | tf_op jit(solution)/shard_map/all_to_all | solution.py:109
  519.1 36.3 %all-to-all-start.2 = ((bf16[16,2,8192]{2,1,0:T(2,128)(2,1)}), bf16[16,2,8192]{2,1,0:T(2,128)(2,1)S(1)}, u32[]{:S(2)}, u32[]{:S(2)}) async-start(bf16[16,2,8192]{2,1,0:T(2,128)(2,1)} %reshape.157), calls=%async_computation.2 | async-start | bytes 1048576 | tf_op jit(solution)/shard_map/all_to_all | solution.py:110
  559.9 152.8 %all-to-all-start.1 = ((bf16[16,2,64,2048]{3,2,1,0:T(8,128)(2,1)}), bf16[16,2,64,2048]{3,2,1,0:T(8,128)(2,1)}, u32[]{:S(2)}, u32[]{:S(2)}) async-start(bf16[16,2,64,2048]{3,2,1,0:T(8,128)(2,1)} %stack.14), calls=%async_computation.1 | async-start | bytes 16777216 | tf_op jit(solution)/shard_map/all_to_all | solution.py:112
  566.6 65.0 %all-gather.2.cloned.1.call-start = ((), (), s32[]{:S(2)}) async-start(), calls=%async_computation.3 | async-start | bytes 4718592 | tf_op jit(solution)/shard_map/all_gather | solution.py:120
  727.9 6.6 slice-start
  730.2 4.3 slice-start.1
  730.2 4.3 copy-start.5
  734.5 12.4 %copy-start.8 = (bf16[1,1024,1024]{2,1,0:T(8,128)(2,1)S(1)}, bf16[1,1024,1024]{2,1,0:T(8,128)(2,1)}, u32[]{:S(2)}) copy-start(bf16[1,1024,1024]{2,1,0:T(8,128)(2,1)} %get-tuple-element.8) | copy-start | bytes 6291460
  746.9 7.3 copy-start.6
  746.9 7.3 copy-start.7
  754.2 9.8 %copy-start.4 = (f32[1,2048,1024]{2,1,0:T(8,128)S(1)}, f32[1,2048,1024]{2,1,0:T(8,128)}, u32[]{:S(2)}) copy-start(f32[1,2048,1024]{2,1,0:T(8,128)} %convolution_bitcast_fusion) | copy-start | bytes 25165828
  764.1 6.5 copy-start.1
Sparse Core Ops, SparseCore 0:
  596.8 34.6 all-gather.1
